TPU v7x, 512 devices: a whole 4x4x16 slice. The times are simulated.
512 devices in a mesh: ent: 128 (over x, z, core), rep: 4 (over y).
Axes of the slice: x: 4, y: 4, z: 16, core: 2. Of those that a mesh axis runs over, the one named last changes fastest.
Arguments:
- entity_table: float32 [131072, 200], P('ent'), may hold values from -1.8 to 1.8
- entity_state: float32 [131072], P('ent'), may hold values from 1e-05 to 1
- operators: float32 [256, 200, 200], P('ent'), may hold values from -0.4375 to 0.4375
- operator_state: float32 [256, 200, 200], P('ent'), may hold values from 1 to 100
- sources: int32 [131072], P(('ent', 'rep')), may hold values from 0 to 1023
- destinations: int32 [131072], P(('ent', 'rep')), may hold values from 0 to 1023
- relations: int32 [131072, 1], P(('ent', 'rep')), may hold values from 0 to 255; in each aligned block of 256 rows (0 to 255, 256 to 511, ...) at most 2 rows name the same one
- negatives: int32 [512, 1000], P(('ent', 'rep')), may hold values from 0 to 1023
Outputs:
- new_table: float32 [131072, 200], P('ent')
- new_entity_state: float32 [131072], P('ent')
- new_operators: float32 [256, 200, 200], P('ent')
- new_operator_state: float32 [256, 200, 200], P('ent')
Inputs may be any that keep to these rules, and one draw needn't show every extreme that they name: `relations`: among the 256 edges of one device no relation occurs more than 2 times, and some relation occurs exactly 2 times.
All inputs are finite; a program needn't handle non-finite values.
Results may differ from a plain program's by a relative error of at most 0.0019.
Values may be sent and summed in bfloat16 or wider, within the bound.
A program may use at most 64 MiB of HBM per device.

v0:
```python
import jax
import jax.numpy as jnp
from jax import lax
from jax.sharding import PartitionSpec as P

SPAN = 256
EDGE_DEV = 256
REL_DEV = 2


entity_rate = 0.1
operator_rate = 0.02
epsilon = 1e-06


def passed_along(array, axis, by):
    peers = lax.axis_size(axis)
    return lax.ppermute(array, axis, [(i, (i + by) % peers) for i in range(peers)])


def place_slots(relation_ids, capacity):
    count_edges = relation_ids.shape[0]
    ordering = jnp.argsort(relation_ids, stable=True)
    ranked = relation_ids[ordering]
    leading = jnp.searchsorted(ranked, ranked, side="left")
    within = jnp.arange(count_edges, dtype=jnp.int32) - leading
    position = jnp.zeros((count_edges,), jnp.int32).at[ordering].set(within)
    return relation_ids * capacity + position


def score_grads(transformed, target_ids, negative_ids, table_rows):
    target_rows = jnp.take(table_rows, target_ids, axis=0)
    positive = jnp.sum(transformed.astype(jnp.float32) * target_rows.astype(jnp.float32), axis=-1)
    positive_grad = -jax.nn.sigmoid(-positive)
    width = transformed.shape[1]
    blocks = transformed.reshape(-1, SPAN, width)
    negative_count = negative_ids.shape[1]

    def span_step(running, pieces):
        query_block, negative_block = pieces
        negative_rows = jnp.take(table_rows, negative_block, axis=0)
        scores = lax.dot_general(
            query_block, negative_rows, (((1,), (1,)), ((), ())), preferred_element_type=jnp.float32
        )
        negative_grad = (jax.nn.sigmoid(scores) / negative_count).astype(jnp.bfloat16)
        query_part = jnp.dot(negative_grad, negative_rows, preferred_element_type=jnp.float32)
        row_update = lax.dot_general(
            negative_grad, query_block, (((0,), (0,)), ((), ())), preferred_element_type=jnp.float32
        )
        return (running.at[negative_block].add(row_update), query_part)

    starting = jnp.zeros((table_rows.shape[0], width), jnp.float32)
    negative_total, query_parts = lax.scan(span_step, starting, (blocks, negative_ids))
    query_grad = (
        positive_grad[:, None] * target_rows.astype(jnp.float32) + query_parts.reshape(-1, width)
    ).astype(jnp.bfloat16)
    target_grad = negative_total.at[target_ids].add(
        positive_grad[:, None] * transformed.astype(jnp.float32)
    )
    return (query_grad, target_grad)


def row_adagrad(weights, moments, gradient):
    fresh_moments = moments + jnp.mean(gradient * gradient, axis=-1)
    updated = weights - entity_rate * gradient / (jnp.sqrt(fresh_moments)[:, None] + epsilon)
    return (updated, fresh_moments)


def dense_adagrad(weights, moments, gradient):
    fresh_moments = moments + gradient * gradient
    updated = weights - operator_rate * gradient / (jnp.sqrt(fresh_moments) + epsilon)
    return (updated, fresh_moments)


def shards(
    entity_table,
    entity_state,
    operators,
    operator_state,
    sources,
    destinations,
    relations,
    negatives,
):
    groups = lax.axis_size("ent")
    relation_count = REL_DEV * groups
    capacity = max(2, (2 * EDGE_DEV + relation_count - 1) // relation_count)
    width = entity_table.shape[1]
    table_half = entity_table.astype(jnp.bfloat16)
    operators_half = operators.astype(jnp.bfloat16)
    slot_index = place_slots(relations[:, 0], capacity)
    source_rows = jnp.take(table_half, sources, axis=0)
    outgoing = (
        jnp.zeros((relation_count * capacity, width), jnp.bfloat16).at[slot_index].set(source_rows)
    )
    outgoing = outgoing.reshape(groups, REL_DEV, capacity, width)
    arrived = lax.all_to_all(outgoing, "ent", split_axis=0, concat_axis=0, tiled=True)
    result = jnp.einsum(
        "srmd,rdk->srmk", arrived, operators_half, preferred_element_type=jnp.float32
    ).astype(jnp.bfloat16)
    returned = lax.all_to_all(result, "ent", split_axis=0, concat_axis=0, tiled=True)
    transformed_slots = returned
    transformed = jnp.take(transformed_slots.reshape(-1, width), slot_index, axis=0)
    neighbour_table = passed_along(table_half, "ent", -1)
    query_grad, target_grad = score_grads(transformed, destinations, negatives, neighbour_table)
    home_grad = passed_along(target_grad, "ent", 1)
    grad_slots = (
        jnp.zeros((relation_count * capacity, width), jnp.bfloat16).at[slot_index].set(query_grad)
    )
    grad_slots = grad_slots.reshape(groups, REL_DEV, capacity, width)
    arrived_grads = lax.all_to_all(grad_slots, "ent", split_axis=0, concat_axis=0, tiled=True)
    source_grads = jnp.einsum(
        "srmk,rdk->srmd", arrived_grads, operators_half, preferred_element_type=jnp.float32
    ).astype(jnp.bfloat16)
    returned = lax.all_to_all(source_grads, "ent", split_axis=0, concat_axis=0, tiled=True)
    operator_grad = jnp.einsum(
        "srmd,srmk->rdk", arrived, arrived_grads, preferred_element_type=jnp.float32
    )
    source_grad = jnp.take(returned.reshape(-1, width), slot_index, axis=0)
    entity_grad = (
        jnp.zeros(entity_table.shape, jnp.float32).at[sources].add(source_grad.astype(jnp.float32))
        + home_grad
    )
    total_grad, total_operator = lax.psum((entity_grad, operator_grad), "rep")
    new_table, new_entity_state = row_adagrad(entity_table, entity_state, total_grad)
    new_operators, new_operator_state = dense_adagrad(operators, operator_state, total_operator)
    return (new_table, new_entity_state, new_operators, new_operator_state)


def solution(mesh):
    placed = (
        P("ent", None),
        P("ent"),
        P("ent", None, None),
        P("ent", None, None),
        P(("ent", "rep")),
        P(("ent", "rep")),
        P(("ent", "rep"), None),
        P(("ent", "rep"), None),
    )
    return jax.shard_map(
        shards,
        mesh=mesh,
        in_specs=placed,
        out_specs=(P("ent", None), P("ent"), P("ent", None, None), P("ent", None, None)),
        check_vma=False,
    )
```

profile of v0, /device:TPU:1, one launch (start us, length us, event | category | flops | bytes accessed | tf_op | source)
XLA Modules:
  0.0 250.8 jit_solution(7940581182130050421)
XLA Ops:
  7.2 0.8 compare_and_fusion.3
  8.0 0.7 copy-done
  8.6 3.2 %sort.17 = (s32[256]{0:T(256)}, s32[256]{0:T(256)S(1)}) sort(s32[256]{0:T(256)S(1)} %bitcast.31, s32[256]{0:T(256)S(1)} %iota.7), dimensions={0}, to_apply=%region_0.0 | sort | flops 2048 | bytes 4096 | tf_op jit(solution)/shard_map/jit(argsort)/sort | solution.py:23
  11.8 1.9 gather_fusion.1
  13.8 18.4 %while.30 = (s32[]{:T(128)}, u32[256]{0:T(256)S(1)}, u32[256]{0:T(256)S(1)}, s32[256]{0:T(256)S(1)}, s32[]{:T(128)}, /*index=5*/s32[]{:T(128)}, s32[]{}) while((s32[]{:T(128)}, u32[256]{0:T(256)S(1)}, u32[256]{0:T(256)S(1)}, s32[256]{0:T(256)S(1)}, s32[]{:T(128)}, /*index=5*/s32[]{:T(128)}, s32[]{}) %tuple.50), condition=%wide.region_2.3_spmd.clone, body=%wide.region_1.2_spmd.clone.sunk | while | flops 5636 | bytes 22117 | solution.py:25
  13.8 1.9 gather_fusion
  15.9 1.9 gather_fusion
  17.9 1.9 gather_fusion
  19.9 1.9 gather_fusion
  22.0 1.9 gather_fusion
  24.0 1.9 gather_fusion
  26.1 1.9 gather_fusion
  28.1 1.9 gather_fusion
  30.1 1.9 gather_fusion
  32.2 1.4 scatter_custom_fusion
  34.0 0.6 copy-done.8
  34.6 2.3 scatter_custom_fusion.1
  37.0 0.8 reshape.77
  37.8 20.5 %all-to-all-start = ((bf16[128,2,2,200]{3,2,1,0:T(2,128)(2,1)}), bf16[128,2,2,200]{3,2,1,0:T(2,128)(2,1)S(1)}, u32[]{:S(2)}, u32[]{:S(2)}) async-start(bf16[128,2,2,200]{3,2,1,0:T(2,128)(2,1)} %reshape.77), calls=%async_computation | async-start | bytes 524288 | tf_op jit(solution)/shard_map/all_to_all | solution.py:97
  58.3 2.8 %collective-permute-start = (bf16[1024,200]{1,0:T(8,128)(2,1)S(1)}, bf16[1024,200]{1,0:T(8,128)(2,1)S(1)}, u32[]{:S(2)}, u32[]{:S(2)}) collective-permute-start(bf16[1024,200]{1,0:T(8,128)(2,1)S(1)} %convert_element_type.48), channel_id=1, source_target_pairs={{0,508},{4,0},{8,4},{12,8},{16,12},{20,16},{24,20},{28,24},{32,28}... | collective-permute-start | bytes 1228808 | tf_op jit(solution)/shard_map/ppermute | solution.py:18
  61.1 19.7 %all-to-all-done = bf16[128,2,2,200]{3,2,1,0:T(2,128)(2,1)S(1)} async-done(((bf16[128,2,2,200]{3,2,1,0:T(2,128)(2,1)}), bf16[128,2,2,200]{3,2,1,0:T(2,128)(2,1)S(1)}, u32[]{:S(2)}, u32[]{:S(2)}) %all-to-all-start) | async-done | bytes 204832 | tf_op jit(solution)/shard_map/all_to_all | solution.py:97
  81.3 0.9 copy.32
  82.2 7.3 %all-to-all-start.1 = ((bf16[128,2,2,200]{3,2,1,0:T(2,128)(2,1)}), bf16[128,2,2,200]{3,2,1,0:T(2,128)(2,1)S(1)}, u32[]{:S(2)}, u32[]{:S(2)}) async-start(bf16[128,2,2,200]{3,2,1,0:T(2,128)(2,1)} %copy.32), calls=%async_computation.1 | async-start | bytes 524288 | tf_op jit(solution)/shard_map/all_to_all | solution.py:101
  89.5 0.7 copy-done.7
  90.3 1.2 gather_fusion.4
  91.5 4.1 %gather_fusion.2 = bf16[1000,200]{1,0:T(8,128)(2,1)S(1)} fusion(bf16[1024,200]{1,0:T(8,128)(2,1)S(1)} %collective-permute-done, s32[1024]{0:T(1024)S(1)} %pad_clamp_fusion.2), kind=kCustom, calls=%fused_computation.6 | custom fusion | bytes 804000 | tf_op jit(solution)/shard_map/while/body/eval_jaxpr/jit(_take)/gather | solution.py:41
  95.6 16.5 %all-to-all-done.1 = bf16[128,2,2,200]{3,2,1,0:T(2,128)(2,1)S(1)} async-done(((bf16[128,2,2,200]{3,2,1,0:T(2,128)(2,1)}), bf16[128,2,2,200]{3,2,1,0:T(2,128)(2,1)S(1)}, u32[]{:S(2)}, u32[]{:S(2)}) %all-to-all-start.1) | async-done | bytes 204832 | tf_op jit(solution)/shard_map/all_to_all | solution.py:101
  112.4 1.2 gather_fusion.3
  114.8 1.5 scatter_custom_fusion.4
  116.4 0.8 reshape.79
  117.2 7.3 %all-to-all-start.2 = ((bf16[128,2,2,200]{3,2,1,0:T(2,128)(2,1)}), bf16[128,2,2,200]{3,2,1,0:T(2,128)(2,1)S(1)}, u32[]{:S(2)}, u32[]{:S(2)}) async-start(bf16[128,2,2,200]{3,2,1,0:T(2,128)(2,1)} %reshape.79), calls=%async_computation.2 | async-start | bytes 524288 | tf_op jit(solution)/shard_map/all_to_all | solution.py:111
  124.7 1.3 fusion.31
  126.0 6.3 %scatter_custom_fusion.2 = f32[1024,200]{1,0:T(8,128)S(1)} fusion(s32[1000]{0:T(1024)S(1)} %bitcast.36, f32[1000,200]{1,0:T(8,128)} %fusion.31, f32[]{:T(128)} %constant.101.clone.1), kind=kCustom, calls=%fused_computation.32 | custom fusion | flops 200000 | bytes 819712 | tf_op jit(solution)/shard_map/while/body/eval_jaxpr/scatter-add | solution.py:50
  132.2 2.4 scatter_fusion
  134.6 1.2 copy.37
  135.8 3.5 %collective-permute-start.1 = (f32[1024,200]{0,1:T(8,128)}, f32[1024,200]{0,1:T(8,128)}, u32[]{:S(2)}, u32[]{:S(2)}) collective-permute-start(f32[1024,200]{0,1:T(8,128)} %copy.37), channel_id=1, source_target_pairs={{0,4},{4,8},{8,12},{12,16},{16,20},{20,24},{24,28},{28,32},{32,36}... | collective-permute-start | bytes 2457608 | tf_op jit(solution)/shard_map/ppermute | solution.py:18
  139.4 7.8 %all-to-all-done.2 = bf16[128,2,2,200]{3,2,1,0:T(2,128)(2,1)S(1)} async-done(((bf16[128,2,2,200]{3,2,1,0:T(2,128)(2,1)}), bf16[128,2,2,200]{3,2,1,0:T(2,128)(2,1)S(1)}, u32[]{:S(2)}, u32[]{:S(2)}) %all-to-all-start.2) | async-done | bytes 204832 | tf_op jit(solution)/shard_map/all_to_all | solution.py:111
  147.6 0.9 copy.40
  148.5 7.5 %all-to-all-start.3 = ((bf16[128,2,2,200]{3,2,1,0:T(2,128)(2,1)}), bf16[128,2,2,200]{3,2,1,0:T(2,128)(2,1)S(1)}, u32[]{:S(2)}, u32[]{:S(2)}) async-start(bf16[128,2,2,200]{3,2,1,0:T(2,128)(2,1)} %copy.40), calls=%async_computation.3 | async-start | bytes 524288 | tf_op jit(solution)/shard_map/all_to_all | solution.py:115
  156.0 1.0 convolution_bitcast_fusion
  157.0 1.5 copy.41
  158.5 20.1 %all-to-all-done.3 = bf16[128,2,2,200]{3,2,1,0:T(2,128)(2,1)S(1)} async-done(((bf16[128,2,2,200]{3,2,1,0:T(2,128)(2,1)}), bf16[128,2,2,200]{3,2,1,0:T(2,128)(2,1)S(1)}, u32[]{:S(2)}, u32[]{:S(2)}) %all-to-all-start.3) | async-done | bytes 204832 | tf_op jit(solution)/shard_map/all_to_all | solution.py:115
  178.8 3.2 %scatter_custom_fusion.5 = f32[1024,200]{1,0:T(8,128)S(1)} fusion(f32[1024,200]{1,0:T(8,128)S(1)} %copy.41, s32[256]{0:T(256)S(1)} %compare_select_fusion.3, pred[256]{0:T(512)(128)(4,1)S(1)} %get-tuple-element.133, bf16[]{:T(256)} %constant.112.clone.1, bf16[512,200]{1,0:T(8,128)(2,1)S(1)} %reshape.80, s32[1024]{0:T(1024)S(1)} %pad_clamp_fusion.3), kind=kCustom, calls=%fused_computation.37 | custom fusion | flops 153600 | bytes 1085954 | tf_op jit(solution)/shard_map/scatter-add | solution.py:121
  182.0 1.0 copy-done.1
  183.1 56.1 %all-reduce.3.cloned.1.call-done = (f32[1024,200]{1,0:T(8,128)}, f32[2,200,200]{2,1,0:T(8,128)}) async-done(((f32[1024,200]{1,0:T(8,128)}, f32[2,200,200]{2,1,0:T(8,128)}), (f32[1024,200]{1,0:T(8,128)}, f32[2,200,200]{2,1,0:T(8,128)})) %all-reduce.3.cloned.1.call-update) | async-done | bytes 1139216 | tf_op jit(solution)/shard_map/psum | solution.py:124
  239.2 1.5 multiply_reduce_fusion
  241.6 1.2 copy.45
  242.8 1.1 divide_subtract_fusion.1
  (101 shorter events, 4.7 us)
Async XLA Ops:
  7.2 0.8 copy-start.10
  8.0 0.7 copy-start
  13.8 19.8 %copy-start.4 = (f32[1024,200]{0,1:T(8,128)S(1)}, f32[1024,200]{0,1:T(8,128)}, u32[]{:S(2)}) copy-start(f32[1024,200]{0,1:T(8,128)} %param.14) | copy-start | bytes 2457604
  33.9 0.7 copy-start.8
  37.8 43.3 %copy-start.3 = (f32[2,200,200]{2,1,0:T(8,128)S(1)}, f32[2,200,200]{2,1,0:T(8,128)}, u32[]{:S(2)}) copy-start(f32[2,200,200]{2,1,0:T(8,128)} %param.16) | copy-start | bytes 960004
  37.8 43.0 %all-to-all-start = ((bf16[128,2,2,200]{3,2,1,0:T(2,128)(2,1)}), bf16[128,2,2,200]{3,2,1,0:T(2,128)(2,1)S(1)}, u32[]{:S(2)}, u32[]{:S(2)}) async-start(bf16[128,2,2,200]{3,2,1,0:T(2,128)(2,1)} %reshape.77), calls=%async_computation | async-start | bytes 524288 | tf_op jit(solution)/shard_map/all_to_all | solution.py:97
  58.3 31.9 %collective-permute-start = (bf16[1024,200]{1,0:T(8,128)(2,1)S(1)}, bf16[1024,200]{1,0:T(8,128)(2,1)S(1)}, u32[]{:S(2)}, u32[]{:S(2)}) collective-permute-start(bf16[1024,200]{1,0:T(8,128)(2,1)S(1)} %convert_element_type.48), channel_id=1, source_target_pairs={{0,508},{4,0},{8,4},{12,8},{16,12},{20,16},{24,20},{28,24},{32,28}... | collective-permute-start | bytes 1228808 | tf_op jit(solution)/shard_map/ppermute | solution.py:18
  82.2 29.9 %all-to-all-start.1 = ((bf16[128,2,2,200]{3,2,1,0:T(2,128)(2,1)}), bf16[128,2,2,200]{3,2,1,0:T(2,128)(2,1)S(1)}, u32[]{:S(2)}, u32[]{:S(2)}) async-start(bf16[128,2,2,200]{3,2,1,0:T(2,128)(2,1)} %copy.32), calls=%async_computation.1 | async-start | bytes 524288 | tf_op jit(solution)/shard_map/all_to_all | solution.py:101
  89.5 0.7 copy-start.7
  117.2 29.9 %all-to-all-start.2 = ((bf16[128,2,2,200]{3,2,1,0:T(2,128)(2,1)}), bf16[128,2,2,200]{3,2,1,0:T(2,128)(2,1)S(1)}, u32[]{:S(2)}, u32[]{:S(2)}) async-start(bf16[128,2,2,200]{3,2,1,0:T(2,128)(2,1)} %reshape.79), calls=%async_computation.2 | async-start | bytes 524288 | tf_op jit(solution)/shard_map/all_to_all | solution.py:111
  135.8 21.2 %collective-permute-start.1 = (f32[1024,200]{0,1:T(8,128)}, f32[1024,200]{0,1:T(8,128)}, u32[]{:S(2)}, u32[]{:S(2)}) collective-permute-start(f32[1024,200]{0,1:T(8,128)} %copy.37), channel_id=1, source_target_pairs={{0,4},{4,8},{8,12},{12,16},{16,20},{20,24},{24,28},{28,32},{32,36}... | collective-permute-start | bytes 2457608 | tf_op jit(solution)/shard_map/ppermute | solution.py:18
  148.5 30.1 %all-to-all-start.3 = ((bf16[128,2,2,200]{3,2,1,0:T(2,128)(2,1)}), bf16[128,2,2,200]{3,2,1,0:T(2,128)(2,1)S(1)}, u32[]{:S(2)}, u32[]{:S(2)}) async-start(bf16[128,2,2,200]{3,2,1,0:T(2,128)(2,1)} %copy.40), calls=%async_computation.3 | async-start | bytes 524288 | tf_op jit(solution)/shard_map/all_to_all | solution.py:115
  156.0 83.2 %all-reduce.3.cloned.1.call-start = ((), (), s32[]{:S(2)}) async-start(), calls=%async_computation.4 | async-start | bytes 2916352 | tf_op jit(solution)/shard_map/psum | solution.py:124
  182.0 1.0 copy-start.1
  239.2 2.1 copy-start.2
  239.2 1.5 copy-start.9
  241.6 1.2 copy-start.5
  241.6 1.2 copy-start.6
Sparse Core Ops, SparseCore 0:
  183.2 55.9 all-reduce.2
where the time goes:
time: 251 us
  waiting for transfers between devices  120 us (48%)
  starting transfers between devices  49 us (20%)
  local copies, waits for them, and re-layouts  40.8 us (16%)
  other arithmetic  22 us (9%)
  between operations  14.4 us (6%)
  matrix products  3.75 us (1%)
    psum x1, waiting for transfers between devices, shards(): total_grad, total_operator = lax.psum((entity_grad, operator_grad), 'rep')  56.1 us
    all_to_all x1, starting transfers between devices, shards(): lax.all_to_all(outgoing, 'ent', split_axis=0, concat_axis=0, tiled=True)  20.5 us
    all_to_all x1, waiting for transfers between devices, shards(): lax.all_to_all(source_grads, 'ent', split_axis=0, concat_axis=0, tiled=True)  20.1 us
    all_to_all x1, waiting for transfers between devices, shards(): lax.all_to_all(outgoing, 'ent', split_axis=0, concat_axis=0, tiled=True)  19.7 us
    gather x9, local copies, waits for them, and re-layouts, place_slots(): leading = jnp.searchsorted(ranked, ranked, side='left')  17.5 us
    all_to_all x1, waiting for transfers between devices, shards(): lax.all_to_all(result, 'ent', split_axis=0, concat_axis=0, tiled=True)  16.5 us
    all_to_all x1, waiting for transfers between devices, shards(): lax.all_to_all(grad_slots, 'ent', split_axis=0, concat_axis=0, tiled=True)  7.76 us
    all_to_all x1, starting transfers between devices, shards(): lax.all_to_all(source_grads, 'ent', split_axis=0, concat_axis=0, tiled=True)  7.52 us
  transfers between devices with their start and end apart: 7, of which 5 were waited for; matrix products, arithmetic and copies ran while one was open for 9% of the time, Pallas kernels for 0%

commit v1 on v0

v1 whole, which is shorter than its diff:
```python
import functools

import jax
import jax.numpy as jnp
from jax import lax
from jax.experimental import pallas as pl
from jax.experimental.pallas import tpu as pltpu
from jax.sharding import PartitionSpec as P

MESH = pl.DeviceIdType.MESH
F32 = jnp.float32
BF16 = jnp.bfloat16

D = 200
NEG = 1000
ROWS = 1024
EDGES = 256
PEERS = 128
REPS = 4
DEPTH = 16
HALF = 112

entity_rate = 0.1
operator_rate = 0.02
epsilon = 1e-06


def dot(a, b):
    return jnp.dot(a, b, preferred_element_type=F32)


def dot_nt(a, b):
    return lax.dot_general(a, b, (((1,), (1,)), ((), ())), preferred_element_type=F32)


def one_hot(index, iota):
    return jnp.where(iota == index, 1.0, 0.0).astype(BF16)


def column(row):
    return jnp.transpose(jnp.broadcast_to(row, (128, row.shape[1])))[:, :1]


def places(relation):
    row = jnp.broadcast_to(relation, (EDGES, EDGES))
    col = jnp.transpose(row)
    sub = lax.broadcasted_iota(jnp.int32, (EDGES, EDGES), 0)
    lane = lax.broadcasted_iota(jnp.int32, (EDGES, EDGES), 1)
    same = jnp.where(row == col, 1.0, 0.0)
    before_row = jnp.sum(jnp.where(sub < lane, same, 0.0), axis=0, keepdims=True)
    before_col = jnp.sum(jnp.where(lane < sub, same, 0.0), axis=1, keepdims=True)

    def spot(rel, before):
        slot = rel * 2 + before.astype(jnp.int32)
        return (slot // 4) * 8 + lax.rem(slot, 4)

    return spot(relation, before_row), spot(col[:, :1], before_col)


def spread(place_row):
    iota = lax.broadcasted_iota(jnp.int32, (8 * PEERS, EDGES), 0)
    return one_hot(place_row, iota), one_hot(place_row + 4, iota)


def collect(place_col):
    iota = lax.broadcasted_iota(jnp.int32, (EDGES, 8 * PEERS), 1)
    return one_hot(place_col, iota), one_hot(place_col + 4, iota)


def partner(me, i):
    step = (PEERS - i) // 8
    rest = lax.rem(PEERS - i, 8)
    odd = lax.rem(step, 2)
    hop = odd * ((step + 1) // 2) + (1 - odd) * (DEPTH - step // 2)
    x, z, c = me // (2 * DEPTH), lax.rem(me // 2, DEPTH), lax.rem(me, 2)
    return (lax.rem(x + rest // 2, 4) * DEPTH + lax.rem(z + hop, DEPTH)) * 2 + lax.rem(c + rest, 2)


def exchange(me, source, target, own, from_at, to_at, sends, arrivals):
    def send(i, _):
        peer = partner(me, i)
        pltpu.make_async_remote_copy(
            source.at[from_at(peer)],
            target.at[to_at],
            sends,
            arrivals,
            device_id={"ent": peer},
            device_id_type=MESH,
        ).start()
        return 0

    lax.fori_loop(1, PEERS, send, 0)
    target[own] = source[from_at(me)]


def all_of(ref, count, sends, arrivals, axis, me):
    part = ref.at[pl.ds(0, count)]
    return pltpu.make_async_remote_copy(
        part, part, sends, arrivals, device_id={axis: me}, device_id_type=MESH
    )


def kernel(
    table_ref, state_ref, ops_ref, opstate_ref, src_ref, dst_ref, rel_ref, neg_ref,
    table_out, state_out, ops_out, opstate_out,
    half, ops_half, negs, there_dst, there_rel, there_neg, there_src,
    send1, recv1, send2, recv2, send3, recv3, send4, recv4,
    rows_first, hits, tg_send, tg_recv, tg_all, og_send, og_recv, og_all, sg_all,
    ssem, rsem,
):
    me = lax.axis_index("ent")
    y = lax.axis_index("rep")
    nxt = lax.rem(me + 1, PEERS)
    prev = lax.rem(me + PEERS - 1, PEERS)

    barrier = pltpu.get_barrier_semaphore()

    def greet(i, _):
        pl.semaphore_signal(
            barrier, inc=1, device_id={"ent": lax.rem(me + i, PEERS)}, device_id_type=MESH
        )
        return 0

    lax.fori_loop(1, PEERS, greet, 0)
    for i in range(1, REPS):
        pl.semaphore_signal(
            barrier, inc=1, device_id={"rep": lax.rem(y + i, REPS)}, device_id_type=MESH
        )

    def to_reps(source_at, target_at, sem):
        for i in range(1, REPS):
            other = lax.rem(y + i, REPS)
            pltpu.make_async_remote_copy(
                source_at(other), target_at, ssem.at[sem], rsem.at[sem],
                device_id={"rep": other}, device_id_type=MESH,
            ).start()

    half[...] = jnp.zeros_like(half)
    half[0:D, :] = table_ref[...].astype(BF16)
    ops_half[...] = jnp.zeros_like(ops_half)
    for r in range(2):
        ops_half[r, 0:D, 0:D] = ops_ref[r].astype(BF16)
    negs[...] = jnp.full_like(negs, -1)
    negs[:, 0:NEG] = neg_ref[...]
    there_src[y] = src_ref[...]

    place_row, place_col = places(rel_ref[...])
    low, high = spread(place_row)
    picked = one_hot(src_ref[...], lax.broadcasted_iota(jnp.int32, (ROWS, EDGES), 0))
    source_rows = dot(half[...], picked).astype(BF16)
    send1[...] = (
        (dot_nt(low, source_rows[0:128]) + dot_nt(high, source_rows[128:256]))
        .reshape(PEERS, 8, 128)
        .astype(BF16)
    )

    pl.semaphore_wait(barrier, PEERS - 1 + REPS - 1)

    shifted = [
        pltpu.make_async_remote_copy(
            a, b, ssem.at[k], rsem.at[k], device_id={"ent": nxt}, device_id_type=MESH
        )
        for a, b, k in ((dst_ref, there_dst, 4), (rel_ref, there_rel, 5), (negs, there_neg, 6))
    ]
    for copy in shifted:
        copy.start()
    exchange(me, send1, recv1, me, lambda p: p, me, ssem.at[0], rsem.at[0])
    to_reps(lambda other: src_ref, there_src.at[y], 7)

    def regroup(h):
        i = lax.broadcasted_iota(jnp.int32, (512, 1024), 0)
        place = (lax.rem(i, 256) // 2) * 8 + h * 4 + (i // 256) * 2 + lax.rem(i, 2)
        return one_hot(place, lax.broadcasted_iota(jnp.int32, (512, 1024), 1))

    def ungroup(h):
        i = lax.broadcasted_iota(jnp.int32, (1024, 512), 1)
        place = (lax.rem(i, 256) // 2) * 8 + h * 4 + (i // 256) * 2 + lax.rem(i, 2)
        return one_hot(place, lax.broadcasted_iota(jnp.int32, (1024, 512), 0))

    group = [regroup(0), regroup(1)]
    back = [ungroup(0), ungroup(1)]

    def grouped(ref):
        flat = ref[...].astype(F32).reshape(8 * PEERS, 128).astype(BF16)
        return jnp.concatenate([dot(group[0], flat), dot(group[1], flat)], axis=1)

    def ungrouped(value):
        value = value.astype(BF16)
        return (
            (dot(back[0], value[:, 0:128]) + dot(back[1], value[:, 128:256]))
            .reshape(PEERS, 8, 128)
            .astype(BF16)
        )

    all_of(recv1, PEERS - 1, ssem.at[0], rsem.at[0], "ent", me).wait_recv()
    rows1 = grouped(recv1)
    rows1_half = rows1.astype(BF16)
    send2[...] = ungrouped(
        jnp.concatenate(
            [dot(rows1_half[256 * r : 256 * r + 256], ops_half[r]) for r in range(2)], axis=0
        )
    )
    exchange(
        me, send2, recv2, me, lambda p: lax.rem(p + PEERS - 1, PEERS), me, ssem.at[1], rsem.at[1]
    )
    for r in range(2):
        rows_first[r] = jnp.transpose(rows1[256 * r : 256 * r + 256]).astype(BF16)

    for copy in shifted:
        copy.wait_recv()
    all_of(there_src, REPS - 1, ssem.at[7], rsem.at[7], "rep", y).wait_recv()
    far_row, far_col = places(there_rel[...])
    far_low, far_high = spread(far_row)
    take_low, take_high = collect(far_col)
    wide = lax.broadcasted_iota(jnp.int32, (EDGES, ROWS), 1)
    is_target = column(there_dst[...]) == wide
    for k in range(REPS):
        hits[k] = one_hot(column(there_src[k]), wide)
    named = there_neg[...]
    coarse = one_hot(named >> 7, lax.broadcasted_iota(jnp.int32, (8, ROWS), 0))
    fine = one_hot(named & 127, lax.broadcasted_iota(jnp.int32, (128, ROWS), 0))
    tally = dot_nt(coarse, fine)
    tally = jnp.concatenate([tally[j : j + 1] for j in range(8)], axis=1)

    all_of(recv2, PEERS - 1, ssem.at[1], rsem.at[1], "ent", me).wait_recv()
    flat2 = recv2[...].astype(F32).reshape(8 * PEERS, 128).astype(BF16)
    moved = jnp.concatenate([dot(take_low, flat2), dot(take_high, flat2)], axis=1)
    moved_half = moved.astype(BF16)
    scores = dot(moved_half, half[...])
    positive = jnp.sum(jnp.where(is_target, scores, 0.0), axis=1, keepdims=True)
    positive_grad = -jax.nn.sigmoid(-positive)
    weight = (tally * (jax.nn.sigmoid(scores) * (1.0 / NEG))).astype(BF16)
    target_hot = jnp.where(is_target, 1.0, 0.0).astype(BF16)
    query_grad = positive_grad * dot_nt(target_hot, half[...]) + dot_nt(weight, half[...])
    query_half = query_grad.astype(BF16)
    send3[...] = (
        (dot(far_low, query_half[:, 0:128]) + dot(far_high, query_half[:, 128:256]))
        .reshape(PEERS, 8, 128)
        .astype(BF16)
    )
    exchange(me, send3, recv3, prev, lambda p: p, prev, ssem.at[2], rsem.at[2])

    target_grad = dot(jnp.transpose(moved).astype(BF16), weight) + dot(
        jnp.transpose(positive_grad * moved).astype(BF16), target_hot
    )
    for k in range(REPS):
        tg_send[k] = target_grad[0:D, 256 * k : 256 * k + 256].astype(BF16)
    to_reps(lambda other: tg_send.at[other], tg_recv.at[y], 8)
    take_low, take_high = collect(place_col)
    all_of(tg_recv, REPS - 1, ssem.at[8], rsem.at[8], "rep", y).wait_recv()
    total = tg_send[y].astype(F32)
    for i in range(1, REPS):
        total = total + tg_recv[lax.rem(y + i, REPS)].astype(F32)
    tg_all[y] = total.astype(BF16)
    to_reps(lambda other: tg_all.at[y], tg_all.at[y], 9)

    all_of(recv3, PEERS - 1, ssem.at[2], rsem.at[2], "ent", me).wait_recv()
    rows3 = grouped(recv3).astype(BF16)
    send4[...] = ungrouped(
        jnp.concatenate(
            [dot_nt(rows3[256 * r : 256 * r + 256], ops_half[r]) for r in range(2)], axis=0
        )
    )
    exchange(me, send4, recv4, me, lambda p: p, me, ssem.at[3], rsem.at[3])
    for r in range(2):
        operator_grad = dot(rows_first[r], rows3[256 * r : 256 * r + 256])
        og_send[2 * r] = operator_grad[0:HALF].astype(BF16)
        og_send[2 * r + 1] = operator_grad[HALF : 2 * HALF].astype(BF16)
    to_reps(lambda other: og_send.at[other], og_recv.at[y], 10)
    all_of(og_recv, REPS - 1, ssem.at[10], rsem.at[10], "rep", y).wait_recv()
    total = og_send[y].astype(F32)
    for i in range(1, REPS):
        total = total + og_recv[lax.rem(y + i, REPS)].astype(F32)
    og_all[y] = total.astype(BF16)
    to_reps(lambda other: og_all.at[y], og_all.at[y], 11)
    all_of(og_all, REPS - 1, ssem.at[11], rsem.at[11], "rep", y).wait_recv()
    for r in range(2):
        for part, (low_row, high_row) in enumerate(((0, HALF), (HALF, D))):
            gradient = og_all[2 * r + part][0 : high_row - low_row, 0:D].astype(F32)
            fresh = opstate_ref[r, low_row:high_row, :] + gradient * gradient
            opstate_out[r, low_row:high_row, :] = fresh
            ops_out[r, low_row:high_row, :] = ops_ref[r, low_row:high_row, :] - (
                operator_rate * gradient / (jnp.sqrt(fresh) + epsilon)
            )
    all_of(tg_all, REPS - 1, ssem.at[9], rsem.at[9], "rep", y).wait_recv()

    all_of(recv4, PEERS - 1, ssem.at[3], rsem.at[3], "ent", me).wait_recv()
    flat4 = recv4[...].astype(F32).reshape(8 * PEERS, 128).astype(BF16)
    source_grad = jnp.concatenate([dot(take_low, flat4), dot(take_high, flat4)], axis=1)
    sg_all[y] = jnp.transpose(source_grad)[0:D].astype(BF16)
    to_reps(lambda other: sg_all.at[y], sg_all.at[y], 12)
    all_of(sg_all, REPS - 1, ssem.at[12], rsem.at[12], "rep", y).wait_recv()
    gradient = jnp.concatenate([tg_all[k].astype(F32) for k in range(REPS)], axis=1)
    for k in range(REPS):
        gradient = gradient + dot(sg_all[k], hits[k])
    fresh = state_ref[...] + jnp.sum(gradient * gradient, axis=0, keepdims=True) * (1.0 / D)
    state_out[...] = fresh
    table_out[...] = table_ref[...] - gradient * (entity_rate / (jnp.sqrt(fresh) + epsilon))

    for k, buffer in enumerate((send1, send2, send3, send4)):
        all_of(buffer, PEERS - 1, ssem.at[k], rsem.at[k], "ent", me).wait_send()
    for copy in shifted:
        copy.wait_send()
    for k, buffer in (
        (7, there_src), (8, tg_send), (9, tg_all), (10, og_send), (11, og_all), (12, sg_all)
    ):
        all_of(buffer, REPS - 1, ssem.at[k], rsem.at[k], "rep", y).wait_send()


def shards(
    entity_table,
    entity_state,
    operators,
    operator_state,
    sources,
    destinations,
    relations,
    negatives,
):
    vmem = pl.BlockSpec(memory_space=pltpu.VMEM)
    blocks = pltpu.VMEM((PEERS, 8, 128), BF16)
    table, state, ops, opstate = pl.pallas_call(
        kernel,
        name="step",
        out_shape=(
            jax.ShapeDtypeStruct((D, ROWS), F32),
            jax.ShapeDtypeStruct((1, ROWS), F32),
            jax.ShapeDtypeStruct((2, D, D), F32),
            jax.ShapeDtypeStruct((2, D, D), F32),
        ),
        in_specs=[vmem] * 8,
        out_specs=(vmem,) * 4,
        scratch_shapes=[
            pltpu.VMEM((256, ROWS), BF16),
            pltpu.VMEM((2, 256, 256), BF16),
            pltpu.VMEM((1, ROWS), jnp.int32),
            pltpu.VMEM((1, EDGES), jnp.int32),
            pltpu.VMEM((1, EDGES), jnp.int32),
            pltpu.VMEM((1, ROWS), jnp.int32),
            pltpu.VMEM((REPS, 1, EDGES), jnp.int32),
            *([blocks] * 8),
            pltpu.VMEM((2, 256, 256), BF16),
            pltpu.VMEM((REPS, EDGES, ROWS), BF16),
            *([pltpu.VMEM((REPS, D, 256), BF16)] * 3),
            *([pltpu.VMEM((REPS, HALF, 256), BF16)] * 3),
            pltpu.VMEM((REPS, D, 256), BF16),
            pltpu.SemaphoreType.DMA((13,)),
            pltpu.SemaphoreType.DMA((13,)),
        ],
        compiler_params=pltpu.CompilerParams(
            collective_id=0, has_side_effects=True, vmem_limit_bytes=48 << 20
        ),
    )(
        entity_table.T,
        entity_state.reshape(1, ROWS),
        operators,
        operator_state,
        sources.reshape(1, EDGES),
        destinations.reshape(1, EDGES),
        relations.reshape(1, EDGES),
        negatives,
    )
    return (table.T, state.reshape(ROWS), ops, opstate)


def solution(mesh):
    placed = (
        P("ent", None),
        P("ent"),
        P("ent", None, None),
        P("ent", None, None),
        P(("ent", "rep")),
        P(("ent", "rep")),
        P(("ent", "rep"), None),
        P(("ent", "rep"), None),
    )
    return jax.shard_map(
        shards,
        mesh=mesh,
        in_specs=placed,
        out_specs=(P("ent", None), P("ent"), P("ent", None, None), P("ent", None, None)),
        check_vma=False,
    )
```

time: 251 us -> 105 us (0.42)
  waiting for transfers between devices: 120 us -> 0 us
  Pallas kernels: 0 us -> 95.6 us
  starting transfers between devices: 49 us -> 0 us
  local copies, waits for them, and re-layouts: 40.8 us -> 8.18 us
  other arithmetic: 22 us -> 0 us
  between operations: 14.4 us -> 0.67 us
  matrix products: 3.75 us -> 0 us
    pallas_call x0 -> x1, Pallas kernels: none -> 95.6 us  [shards(): pl.pallas_call(kernel, name='step', out_shape=(jax.ShapeDtypeStruct((D, R...]
    all_to_all x4 -> x0, waiting for transfers between devices: 64 us -> none  [the longest x1 20.1 us: shards(): lax.all_to_all(source_grads, 'ent', split_axis=0, concat_axis=0, tiled=True)]
    psum x1 -> x0, waiting for transfers between devices: 56.1 us -> none  [shards(): total_grad, total_operator = lax.psum((entity_grad, operator_grad), 'rep')]
    all_to_all x4 -> x0, starting transfers between devices: 42.6 us -> none  [the longest x1 20.5 us: shards(): lax.all_to_all(outgoing, 'ent', split_axis=0, concat_axis=0, tiled=True)]
    gather x15 -> x0, local copies, waits for them, and re-layouts: 26 us -> none  [the longest x9 17.5 us: place_slots(): leading = jnp.searchsorted(ranked, ranked, side='left')]
    scatter-add x3 -> x0, other arithmetic: 11.8 us -> none  [the longest x1 6.27 us: span_step(): return (running.at[negative_block].add(row_update), query_part)]
    ppermute x2 -> x0, starting transfers between devices: 6.33 us -> none  [passed_along(): lax.ppermute(array, axis, [(i, (i + by) % peers) for i in range(peers)])]
    dot_general x6 -> x0, matrix products: 3.75 us -> none  [the longest x1 1.29 us: span_step(): lax.dot_general(negative_grad, query_block, (((0,), (0,)), ((), ())), pre...]
  transfers between devices with their start and end apart: 7 -> 0, of which waited for: 5 -> 0; matrix products, arithmetic and copies ran while one was open for 9% -> 0% of each run, Pallas kernels for 0% -> 0%
where the time goes in v1:
time: 105 us; the launch traced here: 104 us
  Pallas kernels  95.6 us (91%)
  local copies, waits for them, and re-layouts  8.18 us (8%)
    pallas_call x1, Pallas kernels, shards(): pl.pallas_call(kernel, name='step', out_shape=(jax.ShapeDtypeStruct((D, R...  95.6 us
    unnamed x20, local copies, waits for them, and re-layouts  8.18 us

profile of v1, /device:TPU:1, one launch (start us, length us, event | category | flops | bytes accessed | tf_op | source)
XLA Modules:
  0.0 104.5 jit_solution(17105439017702317863)
XLA Ops:
  0.6 0.0 copy-start.4
  0.6 0.0 copy-start.3
  0.7 0.0 copy-start.5
  0.7 0.7 copy-done.4
  1.3 0.0 copy-done.3
  1.3 0.0 copy-done.5
  1.3 0.0 copy-start
  1.3 1.1 %copy-done = f32[1024,200]{0,1:T(8,128)S(1)} copy-done((f32[1024,200]{0,1:T(8,128)S(1)}, f32[1024,200]{0,1:T(8,128)}, u32[]{:S(2)}) %copy-start) | copy-done | bytes 819224
  2.5 0.0 copy-start.1
  2.5 1.0 copy-done.1
  3.5 0.0 copy-start.2
  3.5 1.0 copy-done.2
  4.5 0.0 copy-start.6
  4.5 0.7 copy-done.6
  5.2 0.0 copy-start.7
  5.2 0.7 copy-done.7
  5.9 95.6 %step.1 = (f32[200,1024]{1,0:T(8,128)S(1)}, f32[1,1024]{1,0:T(1,128)S(1)}, f32[2,200,200]{2,1,0:T(8,128)S(1)}, f32[2,200,200]{2,1,0:T(8,128)S(1)}) custom-call(f32[200,1024]{1,0:T(8,128)S(1)} %bitcast.8, f32[1,1024]{1,0:T(1,128)S(1)} %bitcast.9, f32[2,200,200]{2,1,0:T(8,128)S(1)} %copy-done.1, f32[2,200,200]{2,1,0:T(8,128)S(1)} %copy-done.2, ...), custom_call_target="tpu_custom_call" | custom-call | tf_op jit(solution)/shard_map/step/pallas_call | solution.py:322
  101.5 0.9 copy.16
  102.4 0.6 copy.17
  103.0 0.8 copy.18
  103.7 0.8 copy.19
Async XLA Ops:
  0.6 0.7 copy-start.4
  0.6 0.7 copy-start.3
  0.7 0.7 copy-start.5
  1.3 1.1 %copy-start = (f32[1024,200]{0,1:T(8,128)S(1)}, f32[1024,200]{0,1:T(8,128)}, u32[]{:S(2)}) copy-start(f32[1024,200]{0,1:T(8,128)} %param.8) | copy-start | bytes 2457604
  2.5 1.0 copy-start.1
  3.5 1.0 copy-start.2
  4.5 0.7 copy-start.6
  5.2 0.7 copy-start.7

commit v2 on v1

v2 whole, which is shorter than its diff:
```python
import jax
import jax.numpy as jnp
from jax import lax
from jax.experimental import pallas as pl
from jax.experimental.pallas import tpu as pltpu
from jax.sharding import PartitionSpec as P

MESH = pl.DeviceIdType.MESH
F32 = jnp.float32
BF16 = jnp.bfloat16

D = 200
NEG = 1000
ROWS = 1024
EDGES = 256
PEERS = 128
REPS = 4
DEPTH = 16
HALF = 112
CHUNKS = 4
BLOCKS = PEERS // CHUNKS
SLOTS = 4 * BLOCKS

entity_rate = 0.1
operator_rate = 0.02
epsilon = 1e-06


def dot(a, b):
    return jnp.dot(a, b, preferred_element_type=F32)


def dot_nt(a, b):
    return lax.dot_general(a, b, (((1,), (1,)), ((), ())), preferred_element_type=F32)


def one_hot(index, shape, axis):
    return jnp.where(lax.broadcasted_iota(jnp.int32, shape, axis) == index, 1.0, 0.0).astype(BF16)


def column(row):
    return jnp.transpose(jnp.broadcast_to(row, (128, row.shape[1])))[:, :1]


def split(device):
    return device // (2 * DEPTH), lax.rem(device // 2, DEPTH), lax.rem(device, 2)


def offset(k):
    step, rest = k // 8, lax.rem(k, 8)
    odd = lax.rem(step, 2)
    hop = odd * (7 - step // 2) + (1 - odd) * (8 + step // 2)
    return rest // 2, hop, lax.rem(rest, 2)


def ahead(device, k):
    x, z, c = split(device)
    dx, dz, dc = offset(k)
    return (lax.rem(x + dx, 4) * DEPTH + lax.rem(z + dz, DEPTH)) * 2 + lax.rem(c + dc, 2)


def behind(device, k):
    x, z, c = split(device)
    dx, dz, dc = offset(k)
    return (lax.rem(x + 4 - dx, 4) * DEPTH + lax.rem(z + DEPTH - dz, DEPTH)) * 2 + lax.rem(
        c + dc, 2
    )


def slot_of(relation, device):
    row = jnp.broadcast_to(relation, (EDGES, EDGES))
    col = jnp.transpose(row)
    sub = lax.broadcasted_iota(jnp.int32, (EDGES, EDGES), 0)
    lane = lax.broadcasted_iota(jnp.int32, (EDGES, EDGES), 1)
    earlier = jnp.sum(
        jnp.where((row == col) & (sub < lane), 1.0, 0.0), axis=0, keepdims=True
    ).astype(jnp.int32)
    x, z, c = split(device)
    owner = relation >> 1
    dx = ((owner >> 5) + 4 - x) & 3
    dz = (((owner >> 1) & 15) + DEPTH - z) & 15
    dc = ((owner & 1) + 2 - c) & 1
    step = jnp.where(dz >= 8, 2 * (dz - 8), 15 - 2 * dz)
    k = step * 8 + dx * 2 + dc
    return (k >> 5) * SLOTS + (relation & 1) * (2 * BLOCKS) + (k & 31) * 2 + earlier


def block_row(i):
    slot = i & 127
    return ((slot & 63) >> 1) * 8 + (i >> 7) * 4 + (slot >> 6) * 2 + (slot & 1)


def step_kernel(
    table_hbm, state_hbm, ops_hbm, opstate_hbm, src_hbm, dst_hbm, rel_hbm, neg_hbm,
    table_out, state_out, ops_out, opstate_out,
    table, state, ops, opstate, src, dst, rel, neg,
    half, ops_half, negs, there_dst, there_rel, there_neg, there_src,
    send1, recv1, send2, recv2, send3, recv3, send4, recv4,
    rows_first, rows_third, moved_all, pulled_all, weights, target_hot, target_rows,
    hits, tg_send, tg_recv, tg_all, og_send, og_recv, og_all, sg_all,
    lsem, ssem, rsem, xsend, xrecv,
):
    me = lax.axis_index("ent")
    y = lax.axis_index("rep")
    nxt = lax.rem(me + 1, PEERS)
    prev = lax.rem(me + PEERS - 1, PEERS)

    loads = [
        pltpu.make_async_copy(a, b, lsem.at[i])
        for i, (a, b) in enumerate(
            (
                (rel_hbm, rel), (src_hbm, src), (dst_hbm, dst),
                (neg_hbm, neg), (table_hbm, table), (ops_hbm, ops),
                (opstate_hbm, opstate), (state_hbm, state),
            )
        )
    ]
    for load in loads:
        load.start()

    barrier = pltpu.get_barrier_semaphore()

    def greet(i, _):
        pl.semaphore_signal(
            barrier, inc=1, device_id={"ent": lax.rem(me + i, PEERS)}, device_id_type=MESH
        )
        return 0

    lax.fori_loop(1, PEERS, greet, 0)
    for i in range(1, REPS):
        pl.semaphore_signal(
            barrier, inc=1, device_id={"rep": lax.rem(y + i, REPS)}, device_id_type=MESH
        )

    def to_reps(source_at, target_at, sem):
        for i in range(1, REPS):
            other = lax.rem(y + i, REPS)
            pltpu.make_async_remote_copy(
                source_at(other), target_at, ssem.at[sem], rsem.at[sem],
                device_id={"rep": other}, device_id_type=MESH,
            ).start()

    def from_reps(ref, sem):
        part = ref.at[pl.ds(0, REPS - 1)]
        return pltpu.make_async_remote_copy(
            part, part, ssem.at[sem], rsem.at[sem], device_id={"rep": y}, device_id_type=MESH
        )

    def send_chunk(phase, g, source, target, peer_of):
        def send(i, _):
            k = g * BLOCKS + i
            peer = peer_of(k)

            @pl.when(peer != me)
            def _():
                pltpu.make_async_remote_copy(
                    source.at[k], target.at[k],
                    xsend.at[phase], xrecv.at[phase * CHUNKS + g],
                    device_id={"ent": peer}, device_id_type=MESH,
                ).start()

            @pl.when(peer == me)
            def _():
                pltpu.make_async_copy(
                    source.at[k], target.at[k], xrecv.at[phase * CHUNKS + g]
                ).start()

            return 0

        lax.fori_loop(0, BLOCKS, send, 0)

    def wait_chunk(phase, g, target):
        part = target.at[pl.ds(g * BLOCKS, BLOCKS)]
        pltpu.make_async_copy(part, part, xrecv.at[phase * CHUNKS + g]).wait()

    for load in loads[:4]:
        load.wait()
    negs[...] = jnp.full_like(negs, -1)
    negs[:, 0:NEG] = neg[...]
    there_src[y] = src[...]
    slots = slot_of(rel[...], me)
    pack = one_hot(
        block_row(lax.broadcasted_iota(jnp.int32, (8 * BLOCKS, 2 * SLOTS), 1)),
        (8 * BLOCKS, 2 * SLOTS), 0,
    )
    unpack = one_hot(
        block_row(lax.broadcasted_iota(jnp.int32, (2 * SLOTS, 8 * BLOCKS), 0)),
        (2 * SLOTS, 8 * BLOCKS), 1,
    )

    def put(ref, g, value):
        value = value.astype(BF16)
        stacked = jnp.concatenate([value[:, 0:128], value[:, 128:256]], axis=0)
        ref[g * BLOCKS : (g + 1) * BLOCKS] = (
            dot(pack, stacked).reshape(BLOCKS, 8, 128).astype(BF16)
        )

    def get(ref, g):
        flat = ref[g * BLOCKS : (g + 1) * BLOCKS].astype(F32).reshape(8 * BLOCKS, 128)
        both = dot(unpack, flat.astype(BF16))
        return jnp.concatenate([both[0:SLOTS], both[SLOTS : 2 * SLOTS]], axis=1)

    picked = one_hot(src[...], (ROWS, EDGES), 0)
    half[...] = jnp.zeros_like(half)
    ops_half[...] = jnp.zeros_like(ops_half)
    loads[4].wait()
    half[0:D, :] = table[...].astype(BF16)
    source_rows = dot(half[...], picked).astype(BF16)
    for g in range(CHUNKS):
        here = one_hot(slots - g * SLOTS, (SLOTS, EDGES), 0)
        put(send1, g, dot_nt(here, source_rows))

    pl.semaphore_wait(barrier, PEERS - 1 + REPS - 1)

    for g in range(CHUNKS):
        send_chunk(0, g, send1, recv1, lambda k: ahead(me, k))
    shifted = [
        pltpu.make_async_remote_copy(
            a, b, ssem.at[i], rsem.at[i], device_id={"ent": nxt}, device_id_type=MESH
        )
        for i, (a, b) in enumerate(((dst, there_dst), (rel, there_rel), (negs, there_neg)))
    ]
    for copy in shifted:
        copy.start()
    to_reps(lambda other: src, there_src.at[y], 3)

    loads[5].wait()
    for r in range(2):
        ops_half[r, 0:D, 0:D] = ops[r].astype(BF16)
    for copy in shifted:
        copy.wait_recv()
    far_slots = slot_of(there_rel[...], prev)
    for g in range(CHUNKS):
        here = (
            lax.broadcasted_iota(jnp.int32, (SLOTS, EDGES), 0) == far_slots - g * SLOTS
        )
        target = (
            jnp.sum(
                jnp.where(here, (there_dst[...] + 1).astype(F32), 0.0), axis=1, keepdims=True
            ).astype(jnp.int32)
            - 1
        )
        hot = one_hot(target, (SLOTS, ROWS), 1)
        target_hot[g * SLOTS : (g + 1) * SLOTS] = hot
    target_rows[...] = dot_nt(target_hot[...], half[...])
    named = there_neg[...]
    coarse = one_hot(named >> 7, (8, ROWS), 0)
    fine = one_hot(named & 127, (128, ROWS), 0)
    tally = dot_nt(coarse, fine) * (1.0 / NEG)
    tally = jnp.concatenate([tally[j : j + 1] for j in range(8)], axis=1)

    for g in range(CHUNKS):
        wait_chunk(0, g, recv1)
        rows = get(recv1, g).astype(BF16)
        put(
            send2, g,
            jnp.concatenate(
                [dot(rows[64 * r : 64 * r + 64], ops_half[r]) for r in range(2)], axis=0
            ),
        )
        send_chunk(1, g, send2, recv2, lambda k: lax.rem(behind(me, k) + 1, PEERS))
        for r in range(2):
            rows_first[r, 64 * g : 64 * g + 64] = rows[64 * r : 64 * r + 64]

    from_reps(there_src, 3).wait_recv()
    for k in range(REPS):
        hits[k] = one_hot(column(there_src[k]), (EDGES, ROWS), 1)

    for g in range(CHUNKS):
        span = slice(g * SLOTS, (g + 1) * SLOTS)
        wait_chunk(1, g, recv2)
        moved = get(recv2, g)
        moved_half = moved.astype(BF16)
        scores = dot(moved_half, half[...])
        positive = jnp.sum(
            jnp.where(target_hot[span] > 0, scores, 0.0), axis=1, keepdims=True
        )
        positive_grad = -jax.nn.sigmoid(-positive)
        weight = (tally * jax.nn.sigmoid(scores)).astype(BF16)
        put(send3, g, positive_grad * target_rows[span] + dot_nt(weight, half[...]))
        send_chunk(2, g, send3, recv3, lambda k: ahead(prev, k))
        weights[span] = weight
        moved_all[span] = moved_half
        pulled_all[span] = (positive_grad * moved).astype(BF16)

    def turned(ref):
        return jnp.transpose(ref.astype(F32)).astype(BF16)

    target_grad = dot(turned(moved_all[...]), weights[...]) + dot(
        turned(pulled_all[...]), target_hot[...]
    )
    for k in range(REPS):
        tg_send[k] = target_grad[0:D, 256 * k : 256 * k + 256].astype(BF16)
    to_reps(lambda other: tg_send.at[other], tg_recv.at[y], 4)

    for g in range(CHUNKS):
        wait_chunk(2, g, recv3)
        rows = get(recv3, g).astype(BF16)
        put(
            send4, g,
            jnp.concatenate(
                [dot_nt(rows[64 * r : 64 * r + 64], ops_half[r]) for r in range(2)], axis=0
            ),
        )
        send_chunk(3, g, send4, recv4, lambda k: behind(me, k))
        for r in range(2):
            rows_third[r, 64 * g : 64 * g + 64] = rows[64 * r : 64 * r + 64]

    def summed(sent, received):
        total = sent[y].astype(F32)
        for i in range(1, REPS):
            total = total + received[lax.rem(y + i, REPS)].astype(F32)
        return total.astype(BF16)

    from_reps(tg_recv, 4).wait_recv()
    tg_all[y] = summed(tg_send, tg_recv)
    to_reps(lambda other: tg_all.at[y], tg_all.at[y], 5)
    for r in range(2):
        operator_grad = dot(turned(rows_first[r]), rows_third[r])
        og_send[2 * r] = operator_grad[0:HALF].astype(BF16)
        og_send[2 * r + 1] = operator_grad[HALF : 2 * HALF].astype(BF16)
    to_reps(lambda other: og_send.at[other], og_recv.at[y], 6)
    slot_col = column(slots)
    takes = [one_hot(slot_col - g * SLOTS, (EDGES, SLOTS), 1) for g in range(CHUNKS)]
    from_reps(og_recv, 6).wait_recv()
    og_all[y] = summed(og_send, og_recv)
    to_reps(lambda other: og_all.at[y], og_all.at[y], 7)

    loads[6].wait()
    loads[7].wait()
    from_reps(og_all, 7).wait_recv()
    for r in range(2):
        for part, (low, high) in enumerate(((0, HALF), (HALF, D))):
            gradient = og_all[2 * r + part][0 : high - low, 0:D].astype(F32)
            fresh = opstate[r, low:high, :] + gradient * gradient
            opstate_out[r, low:high, :] = fresh
            ops_out[r, low:high, :] = ops[r, low:high, :] - (
                operator_rate * gradient / (jnp.sqrt(fresh) + epsilon)
            )
    from_reps(tg_all, 5).wait_recv()

    source_grad = jnp.zeros((EDGES, 256), F32)
    for g in range(CHUNKS):
        wait_chunk(3, g, recv4)
        source_grad = source_grad + dot(takes[g], get(recv4, g).astype(BF16))
    sg_all[y] = jnp.transpose(source_grad)[0:D].astype(BF16)
    to_reps(lambda other: sg_all.at[y], sg_all.at[y], 8)

    gradient = jnp.concatenate([tg_all[k].astype(F32) for k in range(REPS)], axis=1)
    from_reps(sg_all, 8).wait_recv()
    for k in range(REPS):
        gradient = gradient + dot(sg_all[k], hits[k])
    fresh = state[...] + jnp.sum(gradient * gradient, axis=0, keepdims=True) * (1.0 / D)
    state_out[...] = fresh
    table_out[...] = table[...] - gradient * (entity_rate / (jnp.sqrt(fresh) + epsilon))

    for phase, buffer in enumerate((send1, send2, send3, send4)):
        part = buffer.at[pl.ds(0, PEERS - 1)]
        pltpu.make_async_remote_copy(
            part, part, xsend.at[phase], xrecv.at[0], device_id={"ent": me}, device_id_type=MESH
        ).wait_send()
    for copy in shifted:
        copy.wait_send()
    for sem, buffer in enumerate((there_src, tg_send, tg_all, og_send, og_all, sg_all)):
        from_reps(buffer, 3 + sem).wait_send()


def write_kernel(table, state, ops, opstate, table_out, state_out, ops_out, opstate_out, sem):
    copies = [
        pltpu.make_async_copy(a, b, sem.at[i])
        for i, (a, b) in enumerate(
            ((table, table_out), (ops, ops_out), (opstate, opstate_out), (state, state_out))
        )
    ]
    for copy in copies:
        copy.start()
    for copy in copies:
        copy.wait()


def shards(
    entity_table,
    entity_state,
    operators,
    operator_state,
    sources,
    destinations,
    relations,
    negatives,
):
    vmem = pl.BlockSpec(memory_space=pltpu.VMEM)
    hbm = pl.BlockSpec(memory_space=pltpu.HBM)
    blocks = pltpu.VMEM((PEERS, 8, 128), BF16)
    whole = CHUNKS * SLOTS
    flat_table = entity_table.T
    results = (
        jax.ShapeDtypeStruct((D, ROWS), F32),
        jax.ShapeDtypeStruct((1, ROWS), F32),
        jax.ShapeDtypeStruct((2, D, D), F32),
        jax.ShapeDtypeStruct((2, D, D), F32),
    )
    fresh = pl.pallas_call(
        step_kernel,
        name="step",
        out_shape=results,
        in_specs=[hbm] * 8,
        out_specs=(vmem,) * 4,
        scratch_shapes=[
            *(pltpu.VMEM(out.shape, F32) for out in results),
            *([pltpu.VMEM((1, EDGES), jnp.int32)] * 3),
            pltpu.VMEM((1, NEG), jnp.int32),
            pltpu.VMEM((256, ROWS), BF16),
            pltpu.VMEM((2, 256, 256), BF16),
            pltpu.VMEM((1, ROWS), jnp.int32),
            pltpu.VMEM((1, EDGES), jnp.int32),
            pltpu.VMEM((1, EDGES), jnp.int32),
            pltpu.VMEM((1, ROWS), jnp.int32),
            pltpu.VMEM((REPS, 1, EDGES), jnp.int32),
            *([blocks] * 8),
            pltpu.VMEM((2, 256, 256), BF16),
            pltpu.VMEM((2, 256, 256), BF16),
            pltpu.VMEM((whole, 256), BF16),
            pltpu.VMEM((whole, 256), BF16),
            pltpu.VMEM((whole, ROWS), BF16),
            pltpu.VMEM((whole, ROWS), BF16),
            pltpu.VMEM((whole, 256), F32),
            pltpu.VMEM((REPS, EDGES, ROWS), BF16),
            *([pltpu.VMEM((REPS, D, 256), BF16)] * 3),
            *([pltpu.VMEM((REPS, HALF, 256), BF16)] * 3),
            pltpu.VMEM((REPS, D, 256), BF16),
            pltpu.SemaphoreType.DMA((8,)),
            pltpu.SemaphoreType.DMA((9,)),
            pltpu.SemaphoreType.DMA((9,)),
            pltpu.SemaphoreType.DMA((4,)),
            pltpu.SemaphoreType.DMA((4 * CHUNKS,)),
        ],
        compiler_params=pltpu.CompilerParams(
            collective_id=0, has_side_effects=True, vmem_limit_bytes=32 << 20
        ),
    )(
        *(
            pltpu.with_memory_space_constraint(array, pltpu.HBM)
            for array in (
                flat_table,
                entity_state.reshape(1, ROWS),
                operators,
                operator_state,
                sources.reshape(1, EDGES),
                destinations.reshape(1, EDGES),
                relations.reshape(1, EDGES),
                negatives,
            )
        )
    )
    table, state, ops, opstate = pl.pallas_call(
        write_kernel,
        name="write",
        out_shape=results,
        in_specs=[vmem] * 4,
        out_specs=(hbm,) * 4,
        scratch_shapes=[pltpu.SemaphoreType.DMA((4,))],
        compiler_params=pltpu.CompilerParams(vmem_limit_bytes=4 << 20),
    )(*fresh)
    return (table.T, state.reshape(ROWS), ops, opstate)


def solution(mesh):
    placed = (
        P("ent", None),
        P("ent"),
        P("ent", None, None),
        P("ent", None, None),
        P(("ent", "rep")),
        P(("ent", "rep")),
        P(("ent", "rep"), None),
        P(("ent", "rep"), None),
    )
    return jax.shard_map(
        shards,
        mesh=mesh,
        in_specs=placed,
        out_specs=(P("ent", None), P("ent"), P("ent", None, None), P("ent", None, None)),
        check_vma=False,
    )
```

time: 105 us -> 93.2 us (0.89)
  local copies, waits for them, and re-layouts: 8.18 us -> 0 us
  Pallas kernels: 95.6 us -> 91.2 us
    unnamed x20 -> x0, local copies, waits for them, and re-layouts: 8.18 us -> none
    pallas_call x1 -> x2, Pallas kernels: 95.6 us -> 91.2 us  [the longest x1 90 us: shards(): pl.pallas_call(step_kernel, name='step', out_shape=results, in_specs=[hbm...]
where the time goes in v2:
time: 93.2 us; the launch traced here: 91.8 us
  Pallas kernels  91.2 us (98%)
    pallas_call x1, Pallas kernels, shards(): pl.pallas_call(step_kernel, name='step', out_shape=results, in_specs=[hbm...  90 us

profile of v2, /device:TPU:1, one launch (start us, length us, event | category | flops | bytes accessed | tf_op | source)
XLA Modules:
  0.0 91.8 jit_solution(6021718467979919389)
XLA Ops:
  0.6 90.0 %step.1 = (f32[200,1024]{1,0:T(8,128)S(1)}, f32[1,1024]{1,0:T(1,128)S(1)}, f32[2,200,200]{2,1,0:T(8,128)S(1)}, f32[2,200,200]{2,1,0:T(8,128)S(1)}) custom-call(f32[200,1024]{1,0:T(8,128)} %bitcast.7, f32[1,1024]{1,0:T(1,128)} %bitcast.8, f32[2,200,200]{2,1,0:T(8,128)} %ops_hbm.1, f32[2,200,200]{2,1,0:T(8,128)} %opstate_hbm.1, s32[1,256]{1,0:T(1,128)} %bitcast.9, ...), custom_call_target="tpu_custom_call" | custom-call | tf_op jit(solution)/shard_map/step/pallas_call | solution.py:402
  90.6 1.2 %write.1 = (f32[200,1024]{1,0:T(8,128)}, f32[1,1024]{1,0:T(1,128)}, f32[2,200,200]{2,1,0:T(8,128)}, f32[2,200,200]{2,1,0:T(8,128)}) custom-call(f32[200,1024]{1,0:T(8,128)S(1)} %get-tuple-element.12.table, f32[1,1024]{1,0:T(1,128)S(1)} %get-tuple-element.13.state, f32[2,200,200]{2,1,0:T(8,128)S(1)} %get-tuple-element.14.ops, ...), custom_call_target="tpu_custom_call" | custom-call | tf_op jit(solution)/shard_map/write/pallas_call | solution.py:455

commit v3 on v2

--- a/solution.py
+++ b/solution.py
@@ -18,8 +18,11 @@
 DEPTH = 16
 HALF = 112
 CHUNKS = 4
+HOPS = (8, -6, 4, -2, 7, -5, 3, -1, -7, 5, -3, 1, 6, -4, 2, 0)
 BLOCKS = PEERS // CHUNKS
 SLOTS = 4 * BLOCKS
+STEPS = DEPTH // CHUNKS
+GROUP = 2 * BLOCKS
 
 entity_rate = 0.1
 operator_rate = 0.02
@@ -46,25 +49,15 @@
     return device // (2 * DEPTH), lax.rem(device // 2, DEPTH), lax.rem(device, 2)
 
 
-def offset(k):
-    step, rest = k // 8, lax.rem(k, 8)
-    odd = lax.rem(step, 2)
-    hop = odd * (7 - step // 2) + (1 - odd) * (8 + step // 2)
-    return rest // 2, hop, lax.rem(rest, 2)
-
-
-def ahead(device, k):
+def around(device, sign):
     x, z, c = split(device)
-    dx, dz, dc = offset(k)
-    return (lax.rem(x + dx, 4) * DEPTH + lax.rem(z + dz, DEPTH)) * 2 + lax.rem(c + dc, 2)
-
-
-def behind(device, k):
-    x, z, c = split(device)
-    dx, dz, dc = offset(k)
-    return (lax.rem(x + 4 - dx, 4) * DEPTH + lax.rem(z + DEPTH - dz, DEPTH)) * 2 + lax.rem(
-        c + dc, 2
-    )
+    columns = [lax.rem(x + 4 + sign * dx, 4) * (2 * DEPTH) for dx in range(4)]
+
+    def peers(hop, core):
+        low = 2 * lax.rem(z + DEPTH + sign * hop, DEPTH) + lax.rem(c + core, 2)
+        return [column + low for column in columns]
+
+    return peers
 
 
 def slot_of(relation, device):
@@ -80,14 +73,17 @@
     dx = ((owner >> 5) + 4 - x) & 3
     dz = (((owner >> 1) & 15) + DEPTH - z) & 15
     dc = ((owner & 1) + 2 - c) & 1
-    step = jnp.where(dz >= 8, 2 * (dz - 8), 15 - 2 * dz)
+    step = sum(jnp.where(dz == hop % DEPTH, i, 0) for i, hop in enumerate(HOPS))
     k = step * 8 + dx * 2 + dc
-    return (k >> 5) * SLOTS + (relation & 1) * (2 * BLOCKS) + (k & 31) * 2 + earlier
+    return (
+        (k // BLOCKS) * SLOTS + (relation & 1) * (2 * BLOCKS) + (k & (BLOCKS - 1)) * 2 + earlier
+    )
 
 
 def block_row(i):
-    slot = i & 127
-    return ((slot & 63) >> 1) * 8 + (i >> 7) * 4 + (slot >> 6) * 2 + (slot & 1)
+    slot = i & (SLOTS - 1)
+    pair = slot & (2 * BLOCKS - 1)
+    return (pair >> 1) * 8 + (i // SLOTS) * 4 + (slot // (2 * BLOCKS)) * 2 + (slot & 1)
 
 
 def step_kernel(
@@ -105,6 +101,8 @@
     nxt = lax.rem(me + 1, PEERS)
     prev = lax.rem(me + PEERS - 1, PEERS)
 
+    onward, backward, onward_prev = around(me, 1), around(me, -1), around(prev, 1)
+
     loads = [
         pltpu.make_async_copy(a, b, lsem.at[i])
         for i, (a, b) in enumerate(
@@ -146,28 +144,37 @@
             part, part, ssem.at[sem], rsem.at[sem], device_id={"rep": y}, device_id_type=MESH
         )
 
-    def send_chunk(phase, g, source, target, peer_of):
-        def send(i, _):
-            k = g * BLOCKS + i
-            peer = peer_of(k)
-
-            @pl.when(peer != me)
-            def _():
-                pltpu.make_async_remote_copy(
-                    source.at[k], target.at[k],
-                    xsend.at[phase], xrecv.at[phase * CHUNKS + g],
-                    device_id={"ent": peer}, device_id_type=MESH,
-                ).start()
-
-            @pl.when(peer == me)
-            def _():
-                pltpu.make_async_copy(
-                    source.at[k], target.at[k], xrecv.at[phase * CHUNKS + g]
-                ).start()
-
+    def send_chunk(phase, g, source, target, peers, late=0, fixed=True):
+        def send(core, _):
+            for step in range(g * STEPS, (g + 1) * STEPS):
+                for dx, peer in enumerate(peers(HOPS[step], core)):
+                    k = step * 8 + dx * 2 + core
+                    if late:
+                        peer = lax.rem(peer + late, PEERS)
+
+                    def away(k=k, peer=peer):
+                        pltpu.make_async_remote_copy(
+                            source.at[k], target.at[k],
+                            xsend.at[phase], xrecv.at[phase * CHUNKS + g],
+                            device_id={"ent": peer}, device_id_type=MESH,
+                        ).start()
+
+                    def home(k=k):
+                        pltpu.make_async_copy(
+                            source.at[k], target.at[k], xrecv.at[phase * CHUNKS + g]
+                        ).start()
+
+                    if not fixed and HOPS[step] in (0, 1, -1):
+                        pl.when(peer != me)(away)
+                        pl.when(peer == me)(home)
+                    elif fixed and dx == 0 and HOPS[step] == 0:
+                        pl.when(core == 1)(away)
+                        pl.when(core == 0)(home)
+                    else:
+                        away()
             return 0
 
-        lax.fori_loop(0, BLOCKS, send, 0)
+        lax.fori_loop(0, 2, send, 0)
 
     def wait_chunk(phase, g, target):
         part = target.at[pl.ds(g * BLOCKS, BLOCKS)]
@@ -212,8 +219,6 @@
 
     pl.semaphore_wait(barrier, PEERS - 1 + REPS - 1)
 
-    for g in range(CHUNKS):
-        send_chunk(0, g, send1, recv1, lambda k: ahead(me, k))
     shifted = [
         pltpu.make_async_remote_copy(
             a, b, ssem.at[i], rsem.at[i], device_id={"ent": nxt}, device_id_type=MESH
@@ -224,9 +229,24 @@
         copy.start()
     to_reps(lambda other: src, there_src.at[y], 3)
 
+    for g in range(CHUNKS):
+        send_chunk(0, g, send1, recv1, onward)
     loads[5].wait()
     for r in range(2):
         ops_half[r, 0:D, 0:D] = ops[r].astype(BF16)
+    for g in range(CHUNKS):
+        wait_chunk(0, g, recv1)
+        rows = get(recv1, g).astype(BF16)
+        put(
+            send2, g,
+            jnp.concatenate(
+                [dot(rows[GROUP * r : GROUP * (r + 1)], ops_half[r]) for r in range(2)], axis=0
+            ),
+        )
+        send_chunk(1, g, send2, recv2, backward, late=1, fixed=False)
+        for r in range(2):
+            rows_first[r, GROUP * g : GROUP * (g + 1)] = rows[GROUP * r : GROUP * (r + 1)]
+
     for copy in shifted:
         copy.wait_recv()
     far_slots = slot_of(there_rel[...], prev)
@@ -250,23 +270,6 @@
     tally = jnp.concatenate([tally[j : j + 1] for j in range(8)], axis=1)
 
     for g in range(CHUNKS):
-        wait_chunk(0, g, recv1)
-        rows = get(recv1, g).astype(BF16)
-        put(
-            send2, g,
-            jnp.concatenate(
-                [dot(rows[64 * r : 64 * r + 64], ops_half[r]) for r in range(2)], axis=0
-            ),
-        )
-        send_chunk(1, g, send2, recv2, lambda k: lax.rem(behind(me, k) + 1, PEERS))
-        for r in range(2):
-            rows_first[r, 64 * g : 64 * g + 64] = rows[64 * r : 64 * r + 64]
-
-    from_reps(there_src, 3).wait_recv()
-    for k in range(REPS):
-        hits[k] = one_hot(column(there_src[k]), (EDGES, ROWS), 1)
-
-    for g in range(CHUNKS):
         span = slice(g * SLOTS, (g + 1) * SLOTS)
         wait_chunk(1, g, recv2)
         moved = get(recv2, g)
@@ -278,7 +281,7 @@
         positive_grad = -jax.nn.sigmoid(-positive)
         weight = (tally * jax.nn.sigmoid(scores)).astype(BF16)
         put(send3, g, positive_grad * target_rows[span] + dot_nt(weight, half[...]))
-        send_chunk(2, g, send3, recv3, lambda k: ahead(prev, k))
+        send_chunk(2, g, send3, recv3, onward_prev, fixed=False)
         weights[span] = weight
         moved_all[span] = moved_half
         pulled_all[span] = (positive_grad * moved).astype(BF16)
@@ -299,12 +302,12 @@
         put(
             send4, g,
             jnp.concatenate(
-                [dot_nt(rows[64 * r : 64 * r + 64], ops_half[r]) for r in range(2)], axis=0
+                [dot_nt(rows[GROUP * r : GROUP * (r + 1)], ops_half[r]) for r in range(2)], axis=0
             ),
         )
-        send_chunk(3, g, send4, recv4, lambda k: behind(me, k))
+        send_chunk(3, g, send4, recv4, backward)
         for r in range(2):
-            rows_third[r, 64 * g : 64 * g + 64] = rows[64 * r : 64 * r + 64]
+            rows_third[r, GROUP * g : GROUP * (g + 1)] = rows[GROUP * r : GROUP * (r + 1)]
 
     def summed(sent, received):
         total = sent[y].astype(F32)
@@ -312,22 +315,41 @@
             total = total + received[lax.rem(y + i, REPS)].astype(F32)
         return total.astype(BF16)
 
-    from_reps(tg_recv, 4).wait_recv()
-    tg_all[y] = summed(tg_send, tg_recv)
-    to_reps(lambda other: tg_all.at[y], tg_all.at[y], 5)
     for r in range(2):
         operator_grad = dot(turned(rows_first[r]), rows_third[r])
         og_send[2 * r] = operator_grad[0:HALF].astype(BF16)
         og_send[2 * r + 1] = operator_grad[HALF : 2 * HALF].astype(BF16)
     to_reps(lambda other: og_send.at[other], og_recv.at[y], 6)
+    from_reps(tg_recv, 4).wait_recv()
+    tg_all[y] = summed(tg_send, tg_recv)
+    to_reps(lambda other: tg_all.at[y], tg_all.at[y], 5)
+    from_reps(there_src, 3).wait_recv()
+    for k in range(REPS):
+        hits[k] = one_hot(column(there_src[k]), (EDGES, ROWS), 1)
+
     slot_col = column(slots)
     takes = [one_hot(slot_col - g * SLOTS, (EDGES, SLOTS), 1) for g in range(CHUNKS)]
+    for load in loads[6:]:
+        load.wait()
+
+    source_grad = jnp.zeros((EDGES, 256), F32)
+    for g in range(CHUNKS):
+        wait_chunk(3, g, recv4)
+        source_grad = source_grad + dot(takes[g], get(recv4, g).astype(BF16))
+    sg_all[y] = jnp.transpose(source_grad)[0:D].astype(BF16)
+    to_reps(lambda other: sg_all.at[y], sg_all.at[y], 8)
     from_reps(og_recv, 6).wait_recv()
     og_all[y] = summed(og_send, og_recv)
     to_reps(lambda other: og_all.at[y], og_all.at[y], 7)
 
-    loads[6].wait()
-    loads[7].wait()
+    from_reps(tg_all, 5).wait_recv()
+    gradient = jnp.concatenate([tg_all[k].astype(F32) for k in range(REPS)], axis=1)
+    from_reps(sg_all, 8).wait_recv()
+    for k in range(REPS):
+        gradient = gradient + dot(sg_all[k], hits[k])
+    fresh = state[...] + jnp.sum(gradient * gradient, axis=0, keepdims=True) * (1.0 / D)
+    state_out[...] = fresh
+    table_out[...] = table[...] - gradient * (entity_rate / (jnp.sqrt(fresh) + epsilon))
     from_reps(og_all, 7).wait_recv()
     for r in range(2):
         for part, (low, high) in enumerate(((0, HALF), (HALF, D))):
@@ -337,22 +359,6 @@
             ops_out[r, low:high, :] = ops[r, low:high, :] - (
                 operator_rate * gradient / (jnp.sqrt(fresh) + epsilon)
             )
-    from_reps(tg_all, 5).wait_recv()
-
-    source_grad = jnp.zeros((EDGES, 256), F32)
-    for g in range(CHUNKS):
-        wait_chunk(3, g, recv4)
-        source_grad = source_grad + dot(takes[g], get(recv4, g).astype(BF16))
-    sg_all[y] = jnp.transpose(source_grad)[0:D].astype(BF16)
-    to_reps(lambda other: sg_all.at[y], sg_all.at[y], 8)
-
-    gradient = jnp.concatenate([tg_all[k].astype(F32) for k in range(REPS)], axis=1)
-    from_reps(sg_all, 8).wait_recv()
-    for k in range(REPS):
-        gradient = gradient + dot(sg_all[k], hits[k])
-    fresh = state[...] + jnp.sum(gradient * gradient, axis=0, keepdims=True) * (1.0 / D)
-    state_out[...] = fresh
-    table_out[...] = table[...] - gradient * (entity_rate / (jnp.sqrt(fresh) + epsilon))
 
     for phase, buffer in enumerate((send1, send2, send3, send4)):
         part = buffer.at[pl.ds(0, PEERS - 1)]

time: 93.2 us -> 82.1 us (0.88); the launches traced: 91.8 us -> 82 us
  Pallas kernels: 91.2 us -> 81.4 us
    pallas_call x1, Pallas kernels: 90 us -> 80.2 us  [shards(): pl.pallas_call(step_kernel, name='step', out_shape=results, in_specs=[hbm...]
where the time goes in v3:
time: 82.1 us; the launch traced here: 82 us
  Pallas kernels  81.4 us (99%)
    pallas_call x1, Pallas kernels, shards(): pl.pallas_call(step_kernel, name='step', out_shape=results, in_specs=[hbm...  80.2 us

profile of v3, /device:TPU:1, one launch (start us, length us, event | category | flops | bytes accessed | tf_op | source)
XLA Modules:
  0.0 82.0 jit_solution(5950018062370950202)
XLA Ops:
  0.6 80.2 %step.1 = (f32[200,1024]{1,0:T(8,128)S(1)}, f32[1,1024]{1,0:T(1,128)S(1)}, f32[2,200,200]{2,1,0:T(8,128)S(1)}, f32[2,200,200]{2,1,0:T(8,128)S(1)}) custom-call(f32[200,1024]{1,0:T(8,128)} %bitcast.7, f32[1,1024]{1,0:T(1,128)} %bitcast.8, f32[2,200,200]{2,1,0:T(8,128)} %ops_hbm.1, f32[2,200,200]{2,1,0:T(8,128)} %opstate_hbm.1, s32[1,256]{1,0:T(1,128)} %bitcast.9, ...), custom_call_target="tpu_custom_call" | custom-call | tf_op jit(solution)/shard_map/step/pallas_call | solution.py:408
  80.8 1.2 %write.1 = (f32[200,1024]{1,0:T(8,128)}, f32[1,1024]{1,0:T(1,128)}, f32[2,200,200]{2,1,0:T(8,128)}, f32[2,200,200]{2,1,0:T(8,128)}) custom-call(f32[200,1024]{1,0:T(8,128)S(1)} %get-tuple-element.12.table, f32[1,1024]{1,0:T(1,128)S(1)} %get-tuple-element.13.state, f32[2,200,200]{2,1,0:T(8,128)S(1)} %get-tuple-element.14.ops, ...), custom_call_target="tpu_custom_call" | custom-call | tf_op jit(solution)/shard_map/write/pallas_call | solution.py:461

commit v4 on v3

--- a/solution.py
+++ b/solution.py
@@ -94,7 +94,7 @@
     send1, recv1, send2, recv2, send3, recv3, send4, recv4,
     rows_first, rows_third, moved_all, pulled_all, weights, target_hot, target_rows,
     hits, tg_send, tg_recv, tg_all, og_send, og_recv, og_all, sg_all,
-    lsem, ssem, rsem, xsend, xrecv,
+    lsem, ssem, rsem, gsend, grecv, xsend, xrecv,
 ):
     me = lax.axis_index("ent")
     y = lax.axis_index("rep")
@@ -118,13 +118,22 @@
 
     barrier = pltpu.get_barrier_semaphore()
 
-    def greet(i, _):
-        pl.semaphore_signal(
-            barrier, inc=1, device_id={"ent": lax.rem(me + i, PEERS)}, device_id_type=MESH
-        )
+    def greet(core, _):
+        for far in (8, 7, -7, 6, -6, 5, -5, 4, -4, 3, -3, 2, -2, 1, -1, 0):
+            for dx, peer in enumerate(onward(far, core)):
+
+                def signal(peer=peer):
+                    pl.semaphore_signal(
+                        barrier, inc=1, device_id={"ent": peer}, device_id_type=MESH
+                    )
+
+                if far or dx:
+                    signal()
+                else:
+                    pl.when(core == 1)(signal)
         return 0
 
-    lax.fori_loop(1, PEERS, greet, 0)
+    lax.fori_loop(0, 2, greet, 0)
     for i in range(1, REPS):
         pl.semaphore_signal(
             barrier, inc=1, device_id={"rep": lax.rem(y + i, REPS)}, device_id_type=MESH
@@ -143,6 +152,42 @@
         return pltpu.make_async_remote_copy(
             part, part, ssem.at[sem], rsem.at[sem], device_id={"rep": y}, device_id_type=MESH
         )
+
+    class Gather:
+        def __init__(self, ref, rows, cut, base):
+            left, far, right = (lax.rem(y + i, REPS) for i in (3, 2, 1))
+            first, rest = pl.ds(0, cut), pl.ds(cut, rows - cut)
+
+            def copy(part, owner, to, i):
+                block = ref.at[owner] if part is None else ref.at[owner, part]
+                return pltpu.make_async_remote_copy(
+                    block, block, gsend.at[base + i], grecv.at[base + i],
+                    device_id={"rep": to}, device_id_type=MESH,
+                )
+
+            self.copies = [
+                copy(first, y, left, 0),
+                copy(rest, y, far, 1),
+                copy(None, y, right, 2),
+                copy(rest, y, left, 3),
+                copy(first, right, left, 4),
+            ]
+
+        def start(self):
+            for each in self.copies[:4]:
+                each.start()
+
+        def relay(self):
+            self.copies[0].wait_recv()
+            self.copies[4].start()
+
+        def arrived(self, *which):
+            for i in which:
+                self.copies[i].wait_recv()
+
+        def done(self):
+            for each in self.copies:
+                each.wait_send()
 
     def send_chunk(phase, g, source, target, peers, late=0, fixed=True):
         def send(core, _):
@@ -295,70 +340,82 @@
     for k in range(REPS):
         tg_send[k] = target_grad[0:D, 256 * k : 256 * k + 256].astype(BF16)
     to_reps(lambda other: tg_send.at[other], tg_recv.at[y], 4)
+    turned_rows = [turned(rows_first[r]) for r in range(2)]
+    targets = Gather(tg_all, D, 96, 0)
+    operators = Gather(og_all, HALF, 64, 5)
+    gradients = Gather(sg_all, D, 96, 10)
+
+    def summed(sent, received):
+        total = sent[y].astype(F32)
+        for i in range(1, REPS):
+            total = total + received[lax.rem(y + i, REPS)].astype(F32)
+        return total.astype(BF16)
 
     for g in range(CHUNKS):
         wait_chunk(2, g, recv3)
         rows = get(recv3, g).astype(BF16)
+        for r in range(2):
+            rows_third[r, GROUP * g : GROUP * (g + 1)] = rows[GROUP * r : GROUP * (r + 1)]
         put(
             send4, g,
             jnp.concatenate(
                 [dot_nt(rows[GROUP * r : GROUP * (r + 1)], ops_half[r]) for r in range(2)], axis=0
             ),
         )
+        if g == CHUNKS - 1:
+            for r in range(2):
+                operator_grad = dot(turned_rows[r], rows_third[r])
+                og_send[2 * r] = operator_grad[0:HALF].astype(BF16)
+                og_send[2 * r + 1] = operator_grad[HALF : 2 * HALF].astype(BF16)
+            to_reps(lambda other: og_send.at[other], og_recv.at[y], 5)
         send_chunk(3, g, send4, recv4, backward)
-        for r in range(2):
-            rows_third[r, GROUP * g : GROUP * (g + 1)] = rows[GROUP * r : GROUP * (r + 1)]
-
-    def summed(sent, received):
-        total = sent[y].astype(F32)
-        for i in range(1, REPS):
-            total = total + received[lax.rem(y + i, REPS)].astype(F32)
-        return total.astype(BF16)
-
-    for r in range(2):
-        operator_grad = dot(turned(rows_first[r]), rows_third[r])
-        og_send[2 * r] = operator_grad[0:HALF].astype(BF16)
-        og_send[2 * r + 1] = operator_grad[HALF : 2 * HALF].astype(BF16)
-    to_reps(lambda other: og_send.at[other], og_recv.at[y], 6)
-    from_reps(tg_recv, 4).wait_recv()
-    tg_all[y] = summed(tg_send, tg_recv)
-    to_reps(lambda other: tg_all.at[y], tg_all.at[y], 5)
+        if g == CHUNKS - 2:
+            from_reps(tg_recv, 4).wait_recv()
+            tg_all[y] = summed(tg_send, tg_recv)
+            targets.start()
+
     from_reps(there_src, 3).wait_recv()
     for k in range(REPS):
         hits[k] = one_hot(column(there_src[k]), (EDGES, ROWS), 1)
-
     slot_col = column(slots)
     takes = [one_hot(slot_col - g * SLOTS, (EDGES, SLOTS), 1) for g in range(CHUNKS)]
     for load in loads[6:]:
         load.wait()
+    targets.relay()
 
     source_grad = jnp.zeros((EDGES, 256), F32)
     for g in range(CHUNKS):
         wait_chunk(3, g, recv4)
         source_grad = source_grad + dot(takes[g], get(recv4, g).astype(BF16))
+        if g == CHUNKS - 3:
+            from_reps(og_recv, 5).wait_recv()
+            og_all[y] = summed(og_send, og_recv)
+            operators.start()
+        if g == CHUNKS - 2:
+            operators.relay()
     sg_all[y] = jnp.transpose(source_grad)[0:D].astype(BF16)
-    to_reps(lambda other: sg_all.at[y], sg_all.at[y], 8)
-    from_reps(og_recv, 6).wait_recv()
-    og_all[y] = summed(og_send, og_recv)
-    to_reps(lambda other: og_all.at[y], og_all.at[y], 7)
-
-    from_reps(tg_all, 5).wait_recv()
+    gradients.start()
+
+    targets.arrived(1, 2, 3, 4)
     gradient = jnp.concatenate([tg_all[k].astype(F32) for k in range(REPS)], axis=1)
-    from_reps(sg_all, 8).wait_recv()
-    for k in range(REPS):
-        gradient = gradient + dot(sg_all[k], hits[k])
+    gradient = gradient + dot(sg_all[y], hits[y])
+    gradients.relay()
+    operators.arrived(1, 2, 3, 4)
+    for r in range(2):
+        for part, (low, high) in enumerate(((0, HALF), (HALF, D))):
+            change = og_all[2 * r + part][0 : high - low, 0:D].astype(F32)
+            fresh = opstate[r, low:high, :] + change * change
+            opstate_out[r, low:high, :] = fresh
+            ops_out[r, low:high, :] = ops[r, low:high, :] - (
+                operator_rate * change / (jnp.sqrt(fresh) + epsilon)
+            )
+    for i, which in ((3, (2,)), (1, (3,)), (2, (1, 4))):
+        gradients.arrived(*which)
+        other = lax.rem(y + i, REPS)
+        gradient = gradient + dot(sg_all[other], hits[other])
     fresh = state[...] + jnp.sum(gradient * gradient, axis=0, keepdims=True) * (1.0 / D)
     state_out[...] = fresh
     table_out[...] = table[...] - gradient * (entity_rate / (jnp.sqrt(fresh) + epsilon))
-    from_reps(og_all, 7).wait_recv()
-    for r in range(2):
-        for part, (low, high) in enumerate(((0, HALF), (HALF, D))):
-            gradient = og_all[2 * r + part][0 : high - low, 0:D].astype(F32)
-            fresh = opstate[r, low:high, :] + gradient * gradient
-            opstate_out[r, low:high, :] = fresh
-            ops_out[r, low:high, :] = ops[r, low:high, :] - (
-                operator_rate * gradient / (jnp.sqrt(fresh) + epsilon)
-            )
 
     for phase, buffer in enumerate((send1, send2, send3, send4)):
         part = buffer.at[pl.ds(0, PEERS - 1)]
@@ -367,8 +424,10 @@
         ).wait_send()
     for copy in shifted:
         copy.wait_send()
-    for sem, buffer in enumerate((there_src, tg_send, tg_all, og_send, og_all, sg_all)):
+    for sem, buffer in enumerate((there_src, tg_send, og_send)):
         from_reps(buffer, 3 + sem).wait_send()
+    for each in (targets, operators, gradients):
+        each.done()
 
 
 def write_kernel(table, state, ops, opstate, table_out, state_out, ops_out, opstate_out, sem):
@@ -435,8 +494,10 @@
             *([pltpu.VMEM((REPS, HALF, 256), BF16)] * 3),
             pltpu.VMEM((REPS, D, 256), BF16),
             pltpu.SemaphoreType.DMA((8,)),
-            pltpu.SemaphoreType.DMA((9,)),
-            pltpu.SemaphoreType.DMA((9,)),
+            pltpu.SemaphoreType.DMA((6,)),
+            pltpu.SemaphoreType.DMA((6,)),
+            pltpu.SemaphoreType.DMA((15,)),
+            pltpu.SemaphoreType.DMA((15,)),
             pltpu.SemaphoreType.DMA((4,)),
             pltpu.SemaphoreType.DMA((4 * CHUNKS,)),
         ],

time: 82.1 us -> 80 us (0.974)
  Pallas kernels: 81.4 us -> 79.2 us
    pallas_call x1, Pallas kernels: 80.2 us -> 78 us  [shards(): pl.pallas_call(step_kernel, name='step', out_shape=results, in_specs=[hbm...]
where the time goes in v4:
time: 80 us; the launch traced here: 79.9 us
  Pallas kernels  79.2 us (99%)
    pallas_call x1, Pallas kernels, shards(): pl.pallas_call(step_kernel, name='step', out_shape=results, in_specs=[hbm...  78 us

profile of v4, /device:TPU:1, one launch (start us, length us, event | category | flops | bytes accessed | tf_op | source)
XLA Modules:
  0.0 79.9 jit_solution(10904221927641013144)
XLA Ops:
  0.6 78.0 %step.1 = (f32[200,1024]{1,0:T(8,128)S(1)}, f32[1,1024]{1,0:T(1,128)S(1)}, f32[2,200,200]{2,1,0:T(8,128)S(1)}, f32[2,200,200]{2,1,0:T(8,128)S(1)}) custom-call(f32[200,1024]{1,0:T(8,128)} %bitcast.7, f32[1,1024]{1,0:T(1,128)} %bitcast.8, f32[2,200,200]{2,1,0:T(8,128)} %ops_hbm.1, f32[2,200,200]{2,1,0:T(8,128)} %opstate_hbm.1, s32[1,256]{1,0:T(1,128)} %bitcast.9, ...), custom_call_target="tpu_custom_call" | custom-call | tf_op jit(solution)/shard_map/step/pallas_call | solution.py:467
  78.7 1.2 %write.1 = (f32[200,1024]{1,0:T(8,128)}, f32[1,1024]{1,0:T(1,128)}, f32[2,200,200]{2,1,0:T(8,128)}, f32[2,200,200]{2,1,0:T(8,128)}) custom-call(f32[200,1024]{1,0:T(8,128)S(1)} %get-tuple-element.12.table, f32[1,1024]{1,0:T(1,128)S(1)} %get-tuple-element.13.state, f32[2,200,200]{2,1,0:T(8,128)S(1)} %get-tuple-element.14.ops, ...), custom_call_target="tpu_custom_call" | custom-call | tf_op jit(solution)/shard_map/write/pallas_call | solution.py:522
